TPU v7x, 32 devices: a whole 2x2x4 slice. The times are simulated.
32 devices in a mesh: dp: 8 (over y, x, core), sp: 4 (over z).
Axes of the slice: x: 2, y: 2, z: 4, core: 2. Of those that a mesh axis runs over, the one named last changes fastest.
Arguments:
- inputs: bfloat16 [16, 2048, 768], P('dp', 'sp'), may hold values from -6 to 6
- out_grad: bfloat16 [16, 2048, 768], P('dp', 'sp'), may hold values from -6 to 6
- segment_ids: int32 [16, 2048], P('dp'), may hold values from 0 to 7, as said below
- positions: int32 [16, 2048], P('dp'), may hold values from 0 to 1023, as said below
- norm1_gain: bfloat16 [768], replicated, may hold values from 0.5 to 1.5
- norm1_bias: bfloat16 [768], replicated, may hold values from -1.75 to 1.75
- norm2_gain: bfloat16 [768], replicated, may hold values from 0.5 to 1.5
- norm2_bias: bfloat16 [768], replicated, may hold values from -1.75 to 1.75
- query_weight: bfloat16 [768, 768], replicated, may hold values from -0.21875 to 0.21875
- query_bias: bfloat16 [768], replicated, may hold values from -1.75 to 1.75
- key_weight: bfloat16 [768, 64], replicated, may hold values from -0.21875 to 0.21875
- key_bias: bfloat16 [16], replicated, may hold values from -1.75 to 1.75
- value_weight: bfloat16 [768, 64], replicated, may hold values from -0.21875 to 0.21875
- value_bias: bfloat16 [64], replicated, may hold values from -1.75 to 1.75
- output_weight: bfloat16 [768, 768], replicated, may hold values from -2.5 to 2.5
- output_bias: bfloat16 [768], replicated, may hold values from -1.75 to 1.75
- hidden_weight: bfloat16 [768, 3072], replicated, may hold values from -0.21875 to 0.21875
- hidden_bias: bfloat16 [3072], replicated, may hold values from -1.75 to 1.75
- down_weight: bfloat16 [3072, 768], replicated, may hold values from -0.109375 to 0.109375
- down_bias: bfloat16 [768], replicated, may hold values from -1.75 to 1.75
Outputs:
- layer_out: bfloat16 [16, 2048, 768], P('dp', 'sp')
- input_grad: float32 [16, 2048, 768], P('dp', 'sp')
- norm1_gain_grad: float32 [768], P('sp')
- norm1_bias_grad: float32 [768], P('sp')
- norm2_gain_grad: float32 [768], P('sp')
- norm2_bias_grad: float32 [768], P('sp')
- query_weight_grad: float32 [768, 768], P('sp')
- query_bias_grad: float32 [768], P('sp')
- key_weight_grad: float32 [768, 64], P('sp')
- key_bias_grad: float32 [16], P('sp')
- value_weight_grad: float32 [768, 64], P('sp')
- value_bias_grad: float32 [64], P('sp')
- output_weight_grad: float32 [768, 768], P('sp')
- output_bias_grad: float32 [768], P('sp')
- hidden_weight_grad: float32 [768, 3072], P('sp')
- hidden_bias_grad: float32 [3072], P('sp')
- down_weight_grad: float32 [3072, 768], P('sp')
- down_bias_grad: float32 [768], P('sp')
Inputs may be any that keep to these rules, and one draw needn't show every extreme that they name: `segment_ids`: document numbers of a row start at 0 and rise by one at each of its 7 boundaries, so every row holds exactly 8 documents; the first document of every row holds exactly 1024 tokens and each other document fewer. `positions`: each token's place counted from 0 at the first token of its document.
All inputs are finite; a program needn't handle non-finite values.
Results may differ from a plain program's by a relative error of at most 0.0085.
The roundings to bfloat16 on the way count: a program that leaves them out, or rounds other values in their place, can miss the bound.
Values may be sent and summed in bfloat16 or wider, within the bound.
No kernel may reach another device: no remote copies, remote signals or barrier semaphores. Data moves between devices by JAX's collectives and lax.ppermute only.
A program may use at most 256 MiB of HBM per device.

v0:
```python
import jax
import jax.numpy as jnp
from jax import lax
from jax.sharding import PartitionSpec as P

ROT = 16
EPSILON = 1e-05


def norm_forward(token_rows, gain_vec, offset):
    row_mean = jnp.mean(token_rows, -1, keepdims=True)
    centered = token_rows - row_mean
    inverse = lax.rsqrt(jnp.mean(centered * centered, -1, keepdims=True) + EPSILON)
    normed = centered * inverse
    return (normed * gain_vec + offset, normed, inverse)


def norm_backward(grad_out, normed, inverse, gain_vec):
    scaled = grad_out * gain_vec
    inner_sum = jnp.mean(scaled * normed, -1, keepdims=True)
    grad_in = inverse * (scaled - jnp.mean(scaled, -1, keepdims=True) - normed * inner_sum)
    return (grad_in, jnp.sum(grad_out * normed, 0), jnp.sum(grad_out, 0))


def rope_tables(places):
    half_rot = ROT // 2
    frequency = 10000.0 ** (-(jnp.arange(half_rot, dtype=jnp.float32) * 2.0) / ROT)
    angles = places.astype(jnp.float32)[:, None] * frequency[None, :]
    return (jnp.cos(angles), jnp.sin(angles))


def rotate(values_in, cosine, sine_tab):
    half_rot = ROT // 2
    first_part = values_in[..., :half_rot]
    second_part = values_in[..., half_rot:ROT]
    return jnp.concatenate(
        [
            first_part * cosine - second_part * sine_tab,
            second_part * cosine + first_part * sine_tab,
            values_in[..., ROT:],
        ],
        -1,
    )


def times_transposed(matrix_a, matrix_b):
    return lax.dot_general(
        matrix_a, matrix_b, (((1,), (1,)), ((), ())), preferred_element_type=jnp.float32
    )


def transposed_times(matrix_a, matrix_b):
    return lax.dot_general(
        matrix_a, matrix_b, (((0,), (0,)), ((), ())), preferred_element_type=jnp.float32
    )


def block_mask(seg_query, index_query, segments_all, block_start, block_end, key_end):
    key_index = jnp.arange(key_end, dtype=jnp.int32)
    same_doc = seg_query[block_start:block_end][:, None] == segments_all[None, :key_end]
    earlier = key_index[None, :] <= index_query[block_start:block_end][:, None]
    return (same_doc & earlier)[:, None, :]


def attend_forward(queries, keys_all, values_all, seg_query, index_query, segments_all):
    row_count = queries.shape[0]
    head_dim = keys_all.shape[1]
    heads_here = queries.shape[1] // head_dim
    full_len = keys_all.shape[0]
    block_rows = 512
    scale_factor = head_dim ** (-0.5)
    outputs, lse_list = ([], [])
    for block_start in range(0, row_count, block_rows):
        block_end = block_start + block_rows
        key_end = min(full_len, block_end)
        query_block = queries[block_start:block_end].reshape(block_rows, heads_here, head_dim)
        scores = (
            jnp.einsum(
                "qhd,kd->qhk", query_block, keys_all[:key_end], preferred_element_type=jnp.float32
            )
            * scale_factor
        )
        allowed = block_mask(seg_query, index_query, segments_all, block_start, block_end, key_end)
        masked = jnp.where(allowed, scores, -1e30)
        top_score = jnp.max(masked, -1, keepdims=True)
        exponent = jnp.exp(masked - top_score)
        total_weight = jnp.sum(exponent, -1, keepdims=True)
        weights_blk = (exponent / total_weight).astype(jnp.bfloat16)
        out_block = jnp.einsum(
            "qhk,kd->qhd", weights_blk, values_all[:key_end], preferred_element_type=jnp.float32
        )
        outputs.append(out_block.reshape(block_rows, heads_here * head_dim).astype(jnp.bfloat16))
        lse_list.append(top_score + jnp.log(total_weight))
    return (jnp.concatenate(outputs, 0), lse_list)


def attend_backward(
    queries, keys_all, values_all, grad_heads, lse_list, seg_query, index_query, segments_all
):
    row_count = queries.shape[0]
    head_dim = keys_all.shape[1]
    heads_here = queries.shape[1] // head_dim
    full_len = keys_all.shape[0]
    block_rows = 512
    scale_factor = head_dim ** (-0.5)
    grad_query_parts = []
    grad_kv = jnp.zeros((full_len, 2 * head_dim), jnp.float32)
    for block_number, block_start in enumerate(range(0, row_count, block_rows)):
        block_end = block_start + block_rows
        key_end = min(full_len, block_end)
        query_block = queries[block_start:block_end].reshape(block_rows, heads_here, head_dim)
        grad_block = grad_heads[block_start:block_end].reshape(block_rows, heads_here, head_dim)
        scores = (
            jnp.einsum(
                "qhd,kd->qhk", query_block, keys_all[:key_end], preferred_element_type=jnp.float32
            )
            * scale_factor
        )
        allowed = block_mask(seg_query, index_query, segments_all, block_start, block_end, key_end)
        masked = jnp.where(allowed, scores, -1e30)
        probs_f = jnp.exp(masked - lse_list[block_number])
        weights_blk = probs_f.astype(jnp.bfloat16)
        grad_weights = jnp.einsum(
            "qhd,kd->qhk", grad_block, values_all[:key_end], preferred_element_type=jnp.float32
        )
        row_inner = jnp.sum(probs_f * grad_weights, -1, keepdims=True)
        grad_scores = (probs_f * (grad_weights - row_inner)).astype(jnp.bfloat16)
        grad_query_block = (
            jnp.einsum(
                "qhk,kd->qhd", grad_scores, keys_all[:key_end], preferred_element_type=jnp.float32
            )
            * scale_factor
        )
        grad_key_part = (
            jnp.einsum("qhk,qhd->kd", grad_scores, query_block, preferred_element_type=jnp.float32)
            * scale_factor
        )
        grad_value_part = jnp.einsum(
            "qhk,qhd->kd", weights_blk, grad_block, preferred_element_type=jnp.float32
        )
        grad_kv = grad_kv.at[:key_end].add(jnp.concatenate([grad_key_part, grad_value_part], 1))
        grad_query_parts.append(grad_query_block.reshape(block_rows, heads_here * head_dim))
    return (jnp.concatenate(grad_query_parts, 0), grad_kv)


def gelu_exact(values_in):
    return jax.nn.gelu(values_in, approximate=False)


def one_row(
    token_in,
    grad_in_row,
    segments,
    places_full,
    norm1_gain,
    norm1_bias,
    norm2_gain,
    norm2_bias,
    query_weight,
    query_bias,
    key_weight,
    key_bias,
    value_weight,
    value_bias,
    output_weight,
    output_bias,
    hidden_weight,
    hidden_bias,
    down_weight,
    down_bias,
):
    sp_count = lax.axis_size("sp")
    local_len = token_in.shape[0]
    model_width = token_in.shape[1]
    head_dim = key_weight.shape[1]
    rot_dims = key_bias.shape[0]
    heads_all = model_width // head_dim
    full_len = local_len * sp_count
    start_row = lax.axis_index("sp") * local_len
    places_local = lax.dynamic_slice_in_dim(places_full, start_row, local_len)
    cos_local, sin_local = rope_tables(places_local)
    full_index = jnp.arange(full_len, dtype=jnp.int32)
    token_rows = token_in.astype(jnp.float32)
    norm_one, normed_one, inverse_one = norm_forward(
        token_rows, norm1_gain.astype(jnp.float32), norm1_bias.astype(jnp.float32)
    )
    attn_input = norm_one.astype(jnp.bfloat16)
    key_shift = jnp.concatenate(
        [key_bias.astype(jnp.float32), jnp.zeros((head_dim - rot_dims,), jnp.float32)]
    )
    query_pre = jnp.dot(
        attn_input, query_weight, preferred_element_type=jnp.float32
    ) + query_bias.astype(jnp.float32)
    key_pre = jnp.dot(attn_input, key_weight, preferred_element_type=jnp.float32) + key_shift
    value_pre = jnp.dot(
        attn_input, value_weight, preferred_element_type=jnp.float32
    ) + value_bias.astype(jnp.float32)
    query_rot = rotate(
        query_pre.reshape(local_len, heads_all, head_dim),
        cos_local[:, None, :],
        sin_local[:, None, :],
    )
    query_rot = query_rot.reshape(local_len, model_width).astype(jnp.bfloat16)
    key_rot = rotate(key_pre, cos_local, sin_local).astype(jnp.bfloat16)
    kv_local = jnp.concatenate([key_rot, value_pre.astype(jnp.bfloat16)], 1)
    kv_full = lax.all_gather(kv_local, "sp", axis=0, tiled=True)
    keys_all = kv_full[:, :head_dim]
    values_all = kv_full[:, head_dim:]
    queries = lax.all_to_all(query_rot, "sp", split_axis=1, concat_axis=0, tiled=True)
    heads_out, lse_list = attend_forward(
        queries, keys_all, values_all, segments, full_index, segments
    )
    attn_local = lax.all_to_all(heads_out, "sp", split_axis=0, concat_axis=1, tiled=True)
    attn_branch = jnp.dot(
        attn_local, output_weight, preferred_element_type=jnp.float32
    ) + output_bias.astype(jnp.float32)
    norm_two, normed_two, inverse_two = norm_forward(
        token_rows, norm2_gain.astype(jnp.float32), norm2_bias.astype(jnp.float32)
    )
    mlp_input = norm_two.astype(jnp.bfloat16)
    pre_act = jnp.dot(
        mlp_input, hidden_weight, preferred_element_type=jnp.float32
    ) + hidden_bias.astype(jnp.float32)
    activated, gelu_pull = jax.vjp(gelu_exact, pre_act)
    act_low = activated.astype(jnp.bfloat16)
    mlp_branch = jnp.dot(
        act_low, down_weight, preferred_element_type=jnp.float32
    ) + down_bias.astype(jnp.float32)
    layer_row = (token_rows + attn_branch + mlp_branch).astype(jnp.bfloat16)
    grad_rows_f = grad_in_row.astype(jnp.float32)
    grad_act = times_transposed(grad_in_row, down_weight)
    grad_pre_low = gelu_pull(grad_act)[0].astype(jnp.bfloat16)
    down_weight_grad = transposed_times(act_low, grad_in_row)
    down_bias_grad = jnp.sum(grad_rows_f, 0)
    hidden_weight_grad = transposed_times(mlp_input, grad_pre_low)
    hidden_bias_grad = jnp.sum(grad_pre_low.astype(jnp.float32), 0)
    grad_norm_two = times_transposed(grad_pre_low, hidden_weight)
    mlp_back, norm2_gain_grad, norm2_bias_grad = norm_backward(
        grad_norm_two, normed_two, inverse_two, norm2_gain.astype(jnp.float32)
    )
    grad_attn_low = times_transposed(grad_in_row, output_weight).astype(jnp.bfloat16)
    output_weight_grad = transposed_times(attn_local, grad_in_row)
    grad_heads = lax.all_to_all(grad_attn_low, "sp", split_axis=1, concat_axis=0, tiled=True)
    grad_queries, grad_kv = attend_backward(
        queries, keys_all, values_all, grad_heads, lse_list, segments, full_index, segments
    )
    cos_full, sin_full = rope_tables(places_full)
    heads_here = grad_queries.shape[1] // head_dim
    grad_query_full = rotate(
        grad_queries.reshape(full_len, heads_here, head_dim),
        cos_full[:, None, :],
        -sin_full[:, None, :],
    )
    grad_query_full = grad_query_full.reshape(full_len, heads_here * head_dim).astype(jnp.bfloat16)
    grad_query_local = lax.all_to_all(
        grad_query_full, "sp", split_axis=0, concat_axis=1, tiled=True
    )
    grad_kv_local = lax.psum_scatter(grad_kv, "sp", scatter_dimension=0, tiled=True)
    grad_key_low = rotate(grad_kv_local[:, :head_dim], cos_local, -sin_local).astype(jnp.bfloat16)
    grad_value_low = grad_kv_local[:, head_dim:].astype(jnp.bfloat16)
    query_weight_grad = transposed_times(attn_input, grad_query_local)
    query_bias_grad = jnp.sum(grad_query_local.astype(jnp.float32), 0)
    key_weight_grad = transposed_times(attn_input, grad_key_low)
    key_bias_grad = jnp.sum(grad_key_low[:, :rot_dims].astype(jnp.float32), 0)
    value_weight_grad = transposed_times(attn_input, grad_value_low)
    value_bias_grad = jnp.sum(grad_value_low.astype(jnp.float32), 0)
    grad_norm_one = (
        times_transposed(grad_query_local, query_weight)
        + times_transposed(grad_key_low, key_weight)
        + times_transposed(grad_value_low, value_weight)
    )
    attn_back, norm1_gain_grad, norm1_bias_grad = norm_backward(
        grad_norm_one, normed_one, inverse_one, norm1_gain.astype(jnp.float32)
    )
    input_row = grad_rows_f + attn_back + mlp_back
    grad_list = [
        norm1_gain_grad,
        norm1_bias_grad,
        norm2_gain_grad,
        norm2_bias_grad,
        query_weight_grad,
        query_bias_grad,
        key_weight_grad,
        key_bias_grad,
        value_weight_grad,
        value_bias_grad,
        output_weight_grad,
        down_bias_grad,
        hidden_weight_grad,
        hidden_bias_grad,
        down_weight_grad,
        down_bias_grad,
    ]
    return (layer_row, input_row, grad_list)


def on_device(
    inputs,
    out_grad,
    segment_ids,
    positions,
    norm1_gain,
    norm1_bias,
    norm2_gain,
    norm2_bias,
    query_weight,
    query_bias,
    key_weight,
    key_bias,
    value_weight,
    value_bias,
    output_weight,
    output_bias,
    hidden_weight,
    hidden_bias,
    down_weight,
    down_bias,
):
    sp_count = lax.axis_size("sp")
    params_all = (
        norm1_gain,
        norm1_bias,
        norm2_gain,
        norm2_bias,
        query_weight,
        query_bias,
        key_weight,
        key_bias,
        value_weight,
        value_bias,
        output_weight,
        output_bias,
        hidden_weight,
        hidden_bias,
        down_weight,
        down_bias,
    )
    layer_rows, input_rows = ([], [])
    grad_list = None
    for row_number in range(inputs.shape[0]):
        layer_row, input_row, row_grads = one_row(
            inputs[row_number],
            out_grad[row_number],
            segment_ids[row_number],
            positions[row_number],
            *params_all
        )
        layer_rows.append(layer_row)
        input_rows.append(input_row)
        if grad_list is None:
            grad_list = row_grads
        else:
            grad_list = [total + part for total, part in zip(grad_list, row_grads)]
    layer_out = jnp.stack(layer_rows, 0)
    input_grad = jnp.stack(input_rows, 0)
    flat_parts = [each_grad.reshape(sp_count, -1) for each_grad in grad_list]
    part_sizes = [piece.shape[1] for piece in flat_parts]
    packed = jnp.concatenate(flat_parts, 1)
    own_row = lax.psum_scatter(packed, "sp", scatter_dimension=0, tiled=True)
    summed = lax.psum(own_row, "dp").reshape(-1)
    results = []
    offset_now = 0
    for each_grad, size_now in zip(grad_list, part_sizes):
        shard_shape = (each_grad.shape[0] // sp_count,) + each_grad.shape[1:]
        results.append(summed[offset_now : offset_now + size_now].reshape(shard_shape))
        offset_now = offset_now + size_now
    return (layer_out, input_grad) + tuple(results)


def solution(mesh):
    placed = (
        P("dp", "sp", None),
        P("dp", "sp", None),
        P("dp", None),
        P("dp", None),
        P(),
        P(),
        P(),
        P(),
        P(),
        P(),
        P(),
        P(),
        P(),
        P(),
        P(),
        P(),
        P(),
        P(),
        P(),
        P(),
    )
    return jax.shard_map(
        on_device,
        mesh=mesh,
        in_specs=placed,
        out_specs=(
            P("dp", "sp", None),
            P("dp", "sp", None),
            P("sp"),
            P("sp"),
            P("sp"),
            P("sp"),
            P("sp", None),
            P("sp"),
            P("sp", None),
            P("sp"),
            P("sp", None),
            P("sp"),
            P("sp", None),
            P("sp"),
            P("sp", None),
            P("sp"),
            P("sp", None),
            P("sp"),
        ),
        check_vma=False,
    )
```

profile of v0, /device:TPU:0, one launch (start us, length us, event | category | flops | bytes accessed | tf_op | source)
XLA Modules:
  0.0 1696.9 jit_solution(9105256135938720582)
XLA Ops:
  46.2 16.8 all_gather.7
  77.7 34.7 %multiply_convert_fusion.7 = (bf16[512,3072]{1,0:T(8,128)(2,1)}, f32[512,3072]{1,0:T(8,128)}, bf16[512,3072]{1,0:T(8,128)(2,1)}, f32[512,3072]{1,0:T(8,128)}, f32[512,3072]{1,0:T(8,128)}) fusion(f32[3072]{0:T(1024)S(1)} %copy-done.121, f32[512,3072]{1,0:T(8,128)S(1)} %fusion.278, bf16[768,3072]{1,0:T(8,128)(2,1)S(1)} %bitcast.595, ...), kind=kOutput, calls=%fused_computation.66 | convolution fusion | flops 2625896448 | bytes 36986880 | tf_op jit(solution)/shard_map/dot_general | solution.py:221
  112.5 7.6 convert_reduce_fusion
  120.0 9.0 convert_reduce_fusion.1
  140.2 14.0 reshape.1321
  164.4 12.0 reshape.1322
  202.3 27.9 %all_gather.6 = bf16[2048,128]{0,1:T(8,128)(2,1)S(1)} all-gather(bf16[512,128]{0,1:T(8,128)(2,1)S(1)} %pad_maximum_fusion.10), channel_id=1, replica_groups=mesh['dp'=8,'sp'=4] {'sp'}, dimensions={0}, use_global_device_ids=true | all-gather | bytes 655360 | tf_op jit(solution)/shard_map/all_gather | solution.py:206
  230.2 7.1 fusion.305
  252.7 7.2 all-to-all-done.2
  271.1 9.9 all-to-all-done.6
  370.3 7.8 fusion.157
  381.5 8.6 multiply_reduce_fusion.1
  390.1 9.4 multiply_convert_fusion.1
  438.3 8.3 all-to-all-done.3
  490.3 7.5 fusion.67
  520.3 16.7 all-to-all-done.7
  610.2 13.7 dynamic-update-slice.32
  625.4 49.6 %dynamic-update-slice.34 = f32[4,1501268]{1,0:T(4,128)} dynamic-update-slice(f32[4,1501268]{1,0:T(4,128)} %dynamic-update-slice.33, f32[4,589824]{1,0:T(4,128)} %reshape.1321, s32[]{} %constant.345, s32[]{} %constant.357) | dynamic-update-slice | bytes 18874372
  676.5 49.2 %dynamic-update-slice.36 = f32[4,1501268]{1,0:T(4,128)} dynamic-update-slice(f32[4,1501268]{1,0:T(4,128)} %dynamic-update-slice.35, f32[4,589824]{1,0:T(4,128)} %reshape.1322, s32[]{} %constant.345, s32[]{} %constant.359) | dynamic-update-slice | bytes 18874372
  735.5 788.8 %all-reduce.9.cloned.1.call-done = f32[4,1501268]{1,0:T(4,128)} async-done(((f32[4,1501268]{1,0:T(4,128)}), f32[4,1501268]{1,0:T(4,128)}) %all-reduce.9.cloned.1.call-update) | async-done | bytes 24020304
  1524.2 12.7 constant_dynamic-slice_fusion
  1551.1 86.1 %all-reduce.7.cloned.1.call-done = f32[1,1501268]{1,0:T(1,128)} async-done(((f32[1,1501268]{1,0:T(1,128)}), f32[1,1501268]{1,0:T(1,128)}) %all-reduce.7.cloned.1.call-update) | async-done | bytes 6005088 | tf_op jit(solution)/shard_map/psum | solution.py:360
  1640.0 27.6 %slice_reduce_fusion = (f32[589824]{0:T(1024)}, f32[589824]{0:T(1024)S(1)}) fusion(f32[1,1501268]{1,0:T(1,128)} %all-reduce.7.cloned.1.call-done), kind=kLoop, calls=%fused_computation.133 | loop fusion | bytes 9437184 | tf_op jit(solution)/shard_map/slice | solution.py:365
  1670.9 8.6 slice_reduce_fusion.2
  (574 shorter events, 440.4 us)
Async XLA Ops:
  7.2 26.2 %copy-start = (bf16[768,768]{1,0:T(8,128)(2,1)S(1)}, bf16[768,768]{1,0:T(8,128)(2,1)}, u32[]{:S(2)}) copy-start(bf16[768,768]{1,0:T(8,128)(2,1)} %param.48) | copy-start | bytes 3538948
  10.8 186.0 %all-to-all-start.4 = ((bf16[512,4,192]{0,2,1:T(8,128)(2,1)}), bf16[512,4,192]{0,2,1:T(8,128)(2,1)}, u32[]{:S(2)}, u32[]{:S(2)}) async-start(bf16[512,4,192]{0,2,1:T(8,128)(2,1)} %bitcast.61), calls=%async_computation.4 | async-start | bytes 1572864 | tf_op jit(solution)/shard_map/all_to_all | solution.py:243
  27.9 101.8 %copy-start.85 = (f32[512]{0:T(512)}, f32[512]{0:T(512)S(1)}, u32[]{:S(2)}) copy-start(f32[512]{0:T(512)S(1)} %get-tuple-element.347) | copy-start | bytes 6148
  28.5 101.1 %copy-start.90 = (f32[512]{0:T(512)}, f32[512]{0:T(512)S(1)}, u32[]{:S(2)}) copy-start(f32[512]{0:T(512)S(1)} %add_rsqrt_fusion.1) | copy-start | bytes 6148
  37.3 97.3 %copy-start.71 = (f32[768]{0:T(1024)}, f32[768]{0:T(1024)S(1)}, u32[]{:S(2)}) copy-start(f32[768]{0:T(1024)S(1)} %convert_element_type.350) | copy-start | bytes 9220
  44.3 26.9 %copy-start.115 = (f32[1,512]{1,0:T(1,128)}, f32[1,512]{1,0:T(1,128)S(1)}, u32[]{:S(2)}) copy-start(f32[1,512]{1,0:T(1,128)S(1)} %get-tuple-element.348) | copy-start | bytes 6148
  44.3 26.9 %copy-start.117 = (f32[1,512]{1,0:T(1,128)}, f32[1,512]{1,0:T(1,128)S(1)}, u32[]{:S(2)}) copy-start(f32[1,512]{1,0:T(1,128)S(1)} %get-tuple-element.349) | copy-start | bytes 6148
  72.8 39.6 %slice-start.5 = ((s8[4718592]{0:T(1024)(128)(4,1)}), s8[4194304]{0:T(1024)(128)(4,1)S(1)}, s32[]{:S(2)}) async-start(s8[4718592]{0:T(1024)(128)(4,1)} %bitcast.596), calls=%async_computation.19 | async-start | bytes 8388608
  77.7 34.7 %copy-start.14 = (bf16[2,512,768]{2,1,0:T(8,128)(2,1)S(1)}, bf16[2,512,768]{2,1,0:T(8,128)(2,1)}, u32[]{:S(2)}) copy-start(bf16[2,512,768]{2,1,0:T(8,128)(2,1)} %param.41) | copy-start | bytes 4718596
  77.7 34.7 %slice-start.6 = ((s8[4718592]{0:T(1024)(128)(4,1)}), s8[524288]{0:T(1024)(128)(4,1)S(1)}, s32[]{:S(2)}) async-start(s8[4718592]{0:T(1024)(128)(4,1)} %bitcast.596), calls=%async_computation.20 | async-start | bytes 1048576
  196.8 42.6 %all-to-all-start = ((bf16[512,4,192]{0,2,1:T(8,128)(2,1)}), bf16[512,4,192]{0,2,1:T(8,128)(2,1)S(1)}, u32[]{:S(2)}, u32[]{:S(2)}) async-start(bf16[512,4,192]{0,2,1:T(8,128)(2,1)} %bitcast.4), calls=%async_computation | async-start | bytes 1572864 | tf_op jit(solution)/shard_map/all_to_all | solution.py:209
  240.3 19.7 %all-to-all-start.2 = ((bf16[512,4,192]{0,2,1:T(8,128)(2,1)}), bf16[512,4,192]{0,2,1:T(8,128)(2,1)S(1)}, u32[]{:S(2)}, u32[]{:S(2)}) async-start(bf16[512,4,192]{0,2,1:T(8,128)(2,1)} %bitcast.34), calls=%async_computation.2 | async-start | bytes 1572864 | tf_op jit(solution)/shard_map/all_to_all | solution.py:209
  259.9 21.1 %all-to-all-start.6 = ((bf16[512,4,192]{0,2,1:T(8,128)(2,1)}), bf16[512,4,192]{0,2,1:T(8,128)(2,1)}, u32[]{:S(2)}, u32[]{:S(2)}) async-start(bf16[512,4,192]{0,2,1:T(8,128)(2,1)} %bitcast.80), calls=%async_computation.7 | async-start | bytes 1572864 | tf_op jit(solution)/shard_map/all_to_all | solution.py:243
  316.2 27.9 %copy-start.2 = (f32[512,3,1536]{2,0,1:T(8,128)}, f32[512,3,1536]{2,0,1:T(8,128)S(1)}, u32[]{:S(2)}) copy-start(f32[512,3,1536]{2,0,1:T(8,128)S(1)} %get-tuple-element.312) | copy-start | bytes 28311556
  353.1 57.2 %copy-start.1 = (f32[512,3,2048]{2,0,1:T(8,128)}, f32[512,3,2048]{2,0,1:T(8,128)S(1)}, u32[]{:S(2)}) copy-start(f32[512,3,2048]{2,0,1:T(8,128)S(1)} %get-tuple-element.310) | copy-start | bytes 37748740
  422.5 24.0 %all-to-all-start.3 = ((bf16[4,512,192]{1,2,0:T(8,128)(2,1)}), bf16[4,512,192]{1,2,0:T(8,128)(2,1)S(1)}, u32[]{:S(2)}, u32[]{:S(2)}) async-start(bf16[4,512,192]{1,2,0:T(8,128)(2,1)} %bitcast.510), calls=%async_computation.3 | async-start | bytes 1572864 | tf_op jit(solution)/shard_map/all_to_all | solution.py:213
  426.2 128.1 %reduce-scatter.3.cloned.1.call-start = ((), (), s32[]{:S(2)}) async-start(), calls=%async_computation.10 | async-start | bytes 1310720 | tf_op jit(solution)/shard_map/reduce_scatter | solution.py:258
  446.6 30.7 %all-to-all-start.1 = ((bf16[4,512,192]{1,2,0:T(8,128)(2,1)}), bf16[4,512,192]{1,2,0:T(8,128)(2,1)}, u32[]{:S(2)}, u32[]{:S(2)}) async-start(bf16[4,512,192]{1,2,0:T(8,128)(2,1)} %bitcast.526), calls=%async_computation.1 | async-start | bytes 1572864 | tf_op jit(solution)/shard_map/all_to_all | solution.py:213
  477.3 23.3 %all-to-all-start.5 = ((bf16[4,512,192]{1,2,0:T(8,128)(2,1)}), bf16[4,512,192]{1,2,0:T(8,128)(2,1)S(1)}, u32[]{:S(2)}, u32[]{:S(2)}) async-start(bf16[4,512,192]{1,2,0:T(8,128)(2,1)} %copy.106), calls=%async_computation.5 | async-start | bytes 1572864 | tf_op jit(solution)/shard_map/all_to_all | solution.py:255
  501.5 35.5 %all-to-all-start.7 = ((bf16[4,512,192]{1,2,0:T(8,128)(2,1)}), bf16[4,512,192]{1,2,0:T(8,128)(2,1)S(1)}, u32[]{:S(2)}, u32[]{:S(2)}) async-start(bf16[4,512,192]{1,2,0:T(8,128)(2,1)} %copy.111), calls=%async_computation.8 | async-start | bytes 1572864 | tf_op jit(solution)/shard_map/all_to_all | solution.py:255
  505.0 53.6 %reduce-scatter.5.cloned.1.call-start = ((), (), s32[]{:S(2)}) async-start(), calls=%async_computation.11 | async-start | bytes 1310720 | tf_op jit(solution)/shard_map/reduce_scatter | solution.py:258
  507.7 1016.6 %all-reduce.9.cloned.1.call-start = ((), (), s32[]{:S(2)}) async-start(), calls=%async_computation.13 | async-start | bytes 48041984
  625.4 49.6 %copy-start.105 = (f32[4,768]{1,0:T(4,128)S(1)}, f32[4,768]{1,0:T(4,128)}, u32[]{:S(2)}) copy-start(f32[4,768]{1,0:T(4,128)} %add.500) | copy-start | bytes 36868
  727.2 910.0 %all-reduce.7.cloned.1.call-start = ((), (), s32[]{:S(2)}) async-start(), calls=%async_computation.12 | async-start | bytes 12010496 | tf_op jit(solution)/shard_map/psum | solution.py:360
  (138 other events, 934.7 us)
Sparse Core Ops, SparseCore 0:
  432.3 37.6 reduce-scatter.2
  508.2 33.9 reduce-scatter.4
  727.3 796.9 all-reduce.8
  1537.0 100.1 all-reduce.6
where the time goes:
time: 1710 us; the launch traced here: 1700 us
  waiting for transfers between devices  927 us (54%)
  local copies, waits for them, and re-layouts  289 us (17%)
  matrix products  281 us (16%)
  other arithmetic  104 us (6%)
  blocking collectives  44.7 us (3%)
  starting transfers between devices  35.8 us (2%)
    unnamed x5, waiting for transfers between devices  789 us
    unnamed x319, local copies, waits for them, and re-layouts  155 us
    psum x1, waiting for transfers between devices, on_device(): summed = lax.psum(own_row, 'dp').reshape(-1)  86.1 us
    dot_general x12, matrix products, times_transposed(): lax.dot_general(matrix_a, matrix_b, (((1,), (1,)), ((), ())), preferred_e...  53.4 us
    all_gather x2, blocking collectives, one_row(): kv_full = lax.all_gather(kv_local, 'sp', axis=0, tiled=True)  44.7 us
    slice x7, local copies, waits for them, and re-layouts, on_device(): summed[offset_now:offset_now + size_now].reshape(shard_shape)  42.4 us
    dot_general x12, matrix products, transposed_times(): lax.dot_general(matrix_a, matrix_b, (((0,), (0,)), ((), ())), preferred_e...  41 us
    dot_general x2, matrix products, one_row(): jnp.dot(mlp_input, hidden_weight, preferred_element_type=jnp.float32)  39.5 us
  transfers between devices with their start and end apart: 12, of which 8 were waited for; matrix products, arithmetic and copies ran while one was open for 17% of the time, Pallas kernels for 0%

commit v1 on v0

--- a/solution.py
+++ b/solution.py
@@ -203,7 +203,9 @@
     query_rot = query_rot.reshape(local_len, model_width).astype(jnp.bfloat16)
     key_rot = rotate(key_pre, cos_local, sin_local).astype(jnp.bfloat16)
     kv_local = jnp.concatenate([key_rot, value_pre.astype(jnp.bfloat16)], 1)
-    kv_full = lax.all_gather(kv_local, "sp", axis=0, tiled=True)
+    kv_full = jnp.concatenate(
+        lax.all_to_all(jnp.stack([kv_local] * lax.axis_size("sp")), "sp", 0, 0), axis=0
+    )
     keys_all = kv_full[:, :head_dim]
     values_all = kv_full[:, head_dim:]
     queries = lax.all_to_all(query_rot, "sp", split_axis=1, concat_axis=0, tiled=True)

time: 1710 us -> 1720 us (level)
  blocking collectives: 44.7 us -> 0 us
  waiting for transfers between devices: 927 us -> 962 us
    all_gather x2 -> x0, blocking collectives: 44.7 us -> none  [one_row(): kv_full = lax.all_gather(kv_local, 'sp', axis=0, tiled=True)]
    unnamed x319 -> x323, local copies, waits for them, and re-layouts: 155 us -> 156 us
  transfers between devices with their start and end apart: 12 -> 14, of which waited for: 8 -> 10; matrix products, arithmetic and copies ran while one was open for 17% -> 17% of each run, Pallas kernels for 0% -> 0%
where the time goes in v1:
time: 1720 us; the launch traced here: 1710 us
  waiting for transfers between devices  962 us (56%)
  local copies, waits for them, and re-layouts  297 us (17%)
  matrix products  284 us (17%)
  other arithmetic  107 us (6%)
  starting transfers between devices  45.6 us (3%)
    unnamed x5, waiting for transfers between devices  789 us
    unnamed x323, local copies, waits for them, and re-layouts  156 us
    psum x1, waiting for transfers between devices, on_device(): summed = lax.psum(own_row, 'dp').reshape(-1)  86.1 us
    dot_general x12, matrix products, times_transposed(): lax.dot_general(matrix_a, matrix_b, (((1,), (1,)), ((), ())), preferred_e...  56 us
    slice x7, local copies, waits for them, and re-layouts, on_device(): summed[offset_now:offset_now + size_now].reshape(shard_shape)  42.6 us
    dot_general x12, matrix products, transposed_times(): lax.dot_general(matrix_a, matrix_b, (((0,), (0,)), ((), ())), preferred_e...  41 us
    dot_general x2, matrix products, one_row(): jnp.dot(mlp_input, hidden_weight, preferred_element_type=jnp.float32)  39.6 us
    reshape x6, local copies, waits for them, and re-layouts, on_device(): flat_parts = [each_grad.reshape(sp_count, -1) for each_grad in grad_list]  35.6 us
  transfers between devices with their start and end apart: 14, of which 10 were waited for; matrix products, arithmetic and copies ran while one was open for 17% of the time, Pallas kernels for 0%

profile of v1, /device:TPU:0, one launch (start us, length us, event | category | flops | bytes accessed | tf_op | source)
XLA Modules:
  0.0 1712.0 jit_solution(8673797088254919025)
XLA Ops:
  73.7 34.7 %multiply_convert_fusion.7 = (bf16[512,3072]{1,0:T(8,128)(2,1)}, f32[512,3072]{1,0:T(8,128)}, bf16[512,3072]{1,0:T(8,128)(2,1)}, f32[512,3072]{1,0:T(8,128)}, f32[512,3072]{1,0:T(8,128)}) fusion(f32[3072]{0:T(1024)S(1)} %convert_element_type.353, f32[512,3072]{1,0:T(8,128)S(1)} %fusion.278, bf16[768,3072]{1,0:T(8,128)(2,1)S(1)} %bitcast.632, ...), kind=kOutput, calls=%fused_computation.66 | convolution fusion | flops 2625896448 | bytes 36986880 | tf_op jit(solution)/shard_map/dot_general | solution.py:223
  108.4 7.6 convert_reduce_fusion
  116.0 9.0 convert_reduce_fusion.1
  136.1 14.0 reshape.1333
  160.5 12.1 reshape.1334
  190.1 10.0 all-to-all-done.1
  211.9 11.3 all-to-all-done.6
  238.0 9.2 all-to-all-done
  260.1 10.2 all-to-all-done.3
  281.4 13.1 all-to-all-done.8
  383.7 7.8 fusion.157
  395.0 8.5 multiply_reduce_fusion.1
  403.5 9.4 multiply_convert_fusion.1
  451.7 17.9 %all-to-all-done.5 = bf16[4,512,192]{1,2,0:T(8,128)(2,1)S(1)} async-done(((bf16[4,512,192]{1,2,0:T(8,128)(2,1)}), bf16[4,512,192]{1,2,0:T(8,128)(2,1)S(1)}, u32[]{:S(2)}, u32[]{:S(2)}) %all-to-all-start.5) | async-done | bytes 786464 | tf_op jit(solution)/shard_map/all_to_all | solution.py:215
  508.0 7.5 fusion.67
  536.8 14.6 all-to-all-done.9
  624.6 13.8 dynamic-update-slice.32
  639.8 49.6 %dynamic-update-slice.34 = f32[4,1501268]{1,0:T(4,128)} dynamic-update-slice(f32[4,1501268]{1,0:T(4,128)} %dynamic-update-slice.33, f32[4,589824]{1,0:T(4,128)} %reshape.1333, s32[]{} %constant.345, s32[]{} %constant.357) | dynamic-update-slice | bytes 18874372
  690.9 49.3 %dynamic-update-slice.36 = f32[4,1501268]{1,0:T(4,128)} dynamic-update-slice(f32[4,1501268]{1,0:T(4,128)} %dynamic-update-slice.35, f32[4,589824]{1,0:T(4,128)} %reshape.1334, s32[]{} %constant.345, s32[]{} %constant.359) | dynamic-update-slice | bytes 18874372
  749.9 789.2 %all-reduce.9.cloned.1.call-done = f32[4,1501268]{1,0:T(4,128)} async-done(((f32[4,1501268]{1,0:T(4,128)}), f32[4,1501268]{1,0:T(4,128)}) %all-reduce.9.cloned.1.call-update) | async-done | bytes 24020304
  1539.1 12.7 constant_dynamic-slice_fusion
  1566.0 86.1 %all-reduce.7.cloned.1.call-done = f32[1,1501268]{1,0:T(1,128)} async-done(((f32[1,1501268]{1,0:T(1,128)}), f32[1,1501268]{1,0:T(1,128)}) %all-reduce.7.cloned.1.call-update) | async-done | bytes 6005088 | tf_op jit(solution)/shard_map/psum | solution.py:362
  1654.9 27.6 %slice_reduce_fusion = (f32[589824]{0:T(1024)}, f32[589824]{0:T(1024)S(1)}) fusion(f32[1,1501268]{1,0:T(1,128)} %all-reduce.7.cloned.1.call-done), kind=kLoop, calls=%fused_computation.133 | loop fusion | bytes 9437184 | tf_op jit(solution)/shard_map/slice | solution.py:367
  1685.8 8.6 slice_reduce_fusion.2
  (584 shorter events, 462.5 us)
Async XLA Ops:
  7.2 41.2 %copy-start = (bf16[768,768]{1,0:T(8,128)(2,1)S(1)}, bf16[768,768]{1,0:T(8,128)(2,1)}, u32[]{:S(2)}) copy-start(bf16[768,768]{1,0:T(8,128)(2,1)} %param.48) | copy-start | bytes 3538948
  12.7 112.8 %copy-start.85 = (f32[512]{0:T(512)}, f32[512]{0:T(512)S(1)}, u32[]{:S(2)}) copy-start(f32[512]{0:T(512)S(1)} %get-tuple-element.347) | copy-start | bytes 6148
  12.7 117.8 %copy-start.98 = (f32[512]{0:T(512)}, f32[512]{0:T(512)S(1)}, u32[]{:S(2)}) copy-start(f32[512]{0:T(512)S(1)} %get-tuple-element.346) | copy-start | bytes 6148
  14.7 110.8 %copy-start.90 = (f32[512]{0:T(512)}, f32[512]{0:T(512)S(1)}, u32[]{:S(2)}) copy-start(f32[512]{0:T(512)S(1)} %add_rsqrt_fusion.1) | copy-start | bytes 6148
  14.7 115.8 %copy-start.101 = (f32[512]{0:T(512)}, f32[512]{0:T(512)S(1)}, u32[]{:S(2)}) copy-start(f32[512]{0:T(512)S(1)} %add_rsqrt_fusion) | copy-start | bytes 6148
  25.6 154.6 %all-to-all-start.4 = ((bf16[4,512,128]{1,2,0:T(8,128)(2,1)}), bf16[4,512,128]{1,2,0:T(8,128)(2,1)}, u32[]{:S(2)}, u32[]{:S(2)}) async-start(bf16[4,512,128]{1,2,0:T(8,128)(2,1)} %stack.34), calls=%async_computation.4 | async-start | bytes 1048576 | tf_op jit(solution)/shard_map/all_to_all | solution.py:207
  53.0 77.5 %copy-start.71 = (f32[768]{0:T(1024)}, f32[768]{0:T(1024)S(1)}, u32[]{:S(2)}) copy-start(f32[768]{0:T(1024)S(1)} %convert_element_type.350) | copy-start | bytes 9220
  68.7 39.6 %slice-start.5 = ((s8[4718592]{0:T(1024)(128)(4,1)}), s8[4194304]{0:T(1024)(128)(4,1)S(1)}, s32[]{:S(2)}) async-start(s8[4718592]{0:T(1024)(128)(4,1)} %bitcast.633), calls=%async_computation.21 | async-start | bytes 8388608
  73.6 34.8 %copy-start.15 = (bf16[2,512,768]{2,1,0:T(8,128)(2,1)S(1)}, bf16[2,512,768]{2,1,0:T(8,128)(2,1)}, u32[]{:S(2)}) copy-start(bf16[2,512,768]{2,1,0:T(8,128)(2,1)} %param.41) | copy-start | bytes 4718596
  181.1 19.0 %all-to-all-start.1 = ((bf16[4,512,128]{1,2,0:T(8,128)(2,1)}), bf16[4,512,128]{1,2,0:T(8,128)(2,1)S(1)}, u32[]{:S(2)}, u32[]{:S(2)}) async-start(bf16[4,512,128]{1,2,0:T(8,128)(2,1)} %stack.32), calls=%async_computation.1 | async-start | bytes 1048576 | tf_op jit(solution)/shard_map/all_to_all | solution.py:207
  200.1 23.1 %all-to-all-start.6 = ((bf16[512,4,192]{0,2,1:T(8,128)(2,1)}), bf16[512,4,192]{0,2,1:T(8,128)(2,1)S(1)}, u32[]{:S(2)}, u32[]{:S(2)}) async-start(bf16[512,4,192]{0,2,1:T(8,128)(2,1)} %bitcast.61), calls=%async_computation.6 | async-start | bytes 1572864 | tf_op jit(solution)/shard_map/all_to_all | solution.py:245
  223.1 24.1 %all-to-all-start = ((bf16[512,4,192]{0,2,1:T(8,128)(2,1)}), bf16[512,4,192]{0,2,1:T(8,128)(2,1)}, u32[]{:S(2)}, u32[]{:S(2)}) async-start(bf16[512,4,192]{0,2,1:T(8,128)(2,1)} %bitcast.4), calls=%async_computation | async-start | bytes 1572864 | tf_op jit(solution)/shard_map/all_to_all | solution.py:211
  247.2 23.1 %all-to-all-start.3 = ((bf16[512,4,192]{0,2,1:T(8,128)(2,1)}), bf16[512,4,192]{0,2,1:T(8,128)(2,1)S(1)}, u32[]{:S(2)}, u32[]{:S(2)}) async-start(bf16[512,4,192]{0,2,1:T(8,128)(2,1)} %bitcast.34), calls=%async_computation.3 | async-start | bytes 1572864 | tf_op jit(solution)/shard_map/all_to_all | solution.py:211
  270.3 24.3 %all-to-all-start.8 = ((bf16[512,4,192]{0,2,1:T(8,128)(2,1)}), bf16[512,4,192]{0,2,1:T(8,128)(2,1)}, u32[]{:S(2)}, u32[]{:S(2)}) async-start(bf16[512,4,192]{0,2,1:T(8,128)(2,1)} %bitcast.80), calls=%async_computation.9 | async-start | bytes 1572864 | tf_op jit(solution)/shard_map/all_to_all | solution.py:245
  366.5 57.1 %copy-start.1 = (f32[512,3,2048]{2,0,1:T(8,128)}, f32[512,3,2048]{2,0,1:T(8,128)S(1)}, u32[]{:S(2)}) copy-start(f32[512,3,2048]{2,0,1:T(8,128)S(1)} %get-tuple-element.310) | copy-start | bytes 37748740
  436.0 33.6 %all-to-all-start.5 = ((bf16[4,512,192]{1,2,0:T(8,128)(2,1)}), bf16[4,512,192]{1,2,0:T(8,128)(2,1)S(1)}, u32[]{:S(2)}, u32[]{:S(2)}) async-start(bf16[4,512,192]{1,2,0:T(8,128)(2,1)} %bitcast.514), calls=%async_computation.5 | async-start | bytes 1572864 | tf_op jit(solution)/shard_map/all_to_all | solution.py:215
  439.6 129.0 %reduce-scatter.3.cloned.1.call-start = ((), (), s32[]{:S(2)}) async-start(), calls=%async_computation.12 | async-start | bytes 1310720 | tf_op jit(solution)/shard_map/reduce_scatter | solution.py:260
  469.6 23.9 %all-to-all-start.2 = ((bf16[4,512,192]{1,2,0:T(8,128)(2,1)}), bf16[4,512,192]{1,2,0:T(8,128)(2,1)}, u32[]{:S(2)}, u32[]{:S(2)}) async-start(bf16[4,512,192]{1,2,0:T(8,128)(2,1)} %bitcast.562), calls=%async_computation.2 | async-start | bytes 1572864 | tf_op jit(solution)/shard_map/all_to_all | solution.py:215
  493.5 22.4 %all-to-all-start.7 = ((bf16[4,512,192]{1,2,0:T(8,128)(2,1)}), bf16[4,512,192]{1,2,0:T(8,128)(2,1)S(1)}, u32[]{:S(2)}, u32[]{:S(2)}) async-start(bf16[4,512,192]{1,2,0:T(8,128)(2,1)} %copy.108), calls=%async_computation.7 | async-start | bytes 1572864 | tf_op jit(solution)/shard_map/all_to_all | solution.py:257
  516.8 34.5 %all-to-all-start.9 = ((bf16[4,512,192]{1,2,0:T(8,128)(2,1)}), bf16[4,512,192]{1,2,0:T(8,128)(2,1)S(1)}, u32[]{:S(2)}, u32[]{:S(2)}) async-start(bf16[4,512,192]{1,2,0:T(8,128)(2,1)} %copy.113), calls=%async_computation.10 | async-start | bytes 1572864 | tf_op jit(solution)/shard_map/all_to_all | solution.py:257
  521.5 51.4 %reduce-scatter.5.cloned.1.call-start = ((), (), s32[]{:S(2)}) async-start(), calls=%async_computation.13 | async-start | bytes 1310720 | tf_op jit(solution)/shard_map/reduce_scatter | solution.py:260
  524.1 1015.0 %all-reduce.9.cloned.1.call-start = ((), (), s32[]{:S(2)}) async-start(), calls=%async_computation.15 | async-start | bytes 48041984
  639.8 49.6 %copy-start.107 = (f32[4,768]{1,0:T(4,128)S(1)}, f32[4,768]{1,0:T(4,128)}, u32[]{:S(2)}) copy-start(f32[4,768]{1,0:T(4,128)} %add.500) | copy-start | bytes 36868
  741.6 910.5 %all-reduce.7.cloned.1.call-start = ((), (), s32[]{:S(2)}) async-start(), calls=%async_computation.14 | async-start | bytes 12010496 | tf_op jit(solution)/shard_map/psum | solution.py:362
  (142 other events, 1282.8 us)
Sparse Core Ops, SparseCore 0:
  445.7 34.2 reduce-scatter.2
  524.7 30.3 reduce-scatter.4
  741.7 797.3 all-reduce.8
  1551.9 100.1 all-reduce.6
